TPU v7x, 256 devices: a whole 4x4x8 slice. The times are simulated.
256 devices in a mesh: section: 32 (over x, z_lo, core), tensor: 8 (over z_hi, y).
Axes of the slice: x: 4, y: 4, z: 8 (z_hi: 2, z_lo: 4; z = z_hi * 4 + z_lo), core: 2. Of those that a mesh axis runs over, the one named last changes fastest.
Arguments:
- activations: bfloat16 [32, 256, 4096], P('section', 'tensor'), may hold values from -6 to 6
- upstream_grad: bfloat16 [32, 256, 4096], P('section', 'tensor'), may hold values from -6 to 6
- stash_blocks: bfloat16 [32, 256, 4096], P('section', 'tensor'), may hold values from -6 to 6
- guest_blocks: bfloat16 [32, 256, 4096], P('section', 'tensor'), may hold values from -6 to 6
- norm_gain: float32 [32, 4096], P('section'), may hold values from 0.1 to 1.9
- query_weight: bfloat16 [32, 4096, 4096], P('section', None, 'tensor'), may hold values from -2 to 2
- keyval_weight: bfloat16 [32, 4096, 2, 1024], P('section', None, None, 'tensor'), may hold values from -1 to 1
- output_weight: bfloat16 [32, 4096, 4096], P('section', 'tensor'), may hold values from -0.09375 to 0.09375
- evict_marks: int32 [32, 16], replicated, may hold values from 0 to 1, as said below
Outputs:
- next_input: bfloat16 [32, 256, 4096], P('section', 'tensor')
- prev_grad: bfloat16 [32, 256, 4096], P('section', 'tensor')
- kept_stash: bfloat16 [32, 256, 4096], P('section', 'tensor')
- held_blocks: bfloat16 [32, 256, 4096], P('section', 'tensor')
Inputs may be any that keep to these rules, and one draw needn't show every extreme that they name: `evict_marks`: row s marks with 1 the blocks that section s evicts to section 31 - s; a row has at most 8 ones, row 0 exactly 8, rows of the first half of the sections at least 4.
All inputs are finite; a program needn't handle non-finite values.
Results may differ from a plain program's by a relative error of at most 0.012.
Values may be sent and summed in bfloat16 or wider, within the bound.
A program may use at most 64 MiB of HBM per device.

v0:
```python
import jax
import jax.numpy as jnp
from jax import lax
from jax.sharding import PartitionSpec as P

HEADS = 32
KV_HEADS = 8
HEAD_DIM = 128
EPSILON = 1e-05
NEG_LARGE = -1e30


def from_partner(x, axis, bit):
    return lax.ppermute(x, axis, [(i, i ^ 1 << bit) for i in range(lax.axis_size(axis))])


def shifted(x, axis, by):
    peers = lax.axis_size(axis)
    pairs = [(i, i + by) for i in range(peers) if 0 <= i + by < peers]
    return lax.ppermute(x, axis, pairs)


def root_norm(features, gain_row):
    values = features.astype(jnp.float32)
    factor = lax.rsqrt(jnp.mean(values * values, axis=-1, keepdims=True) + EPSILON)
    return values * factor * gain_row


def causal_probs(scores):
    length = scores.shape[-1]
    allowed = jnp.arange(length)[:, None] >= jnp.arange(length)[None, :]
    masked = jnp.where(allowed, scores, NEG_LARGE)
    row_max = jnp.max(masked, axis=-1, keepdims=True)
    raised = jnp.exp(masked - row_max)
    return raised / jnp.sum(raised, axis=-1, keepdims=True)


def local(
    activations,
    upstream_grad,
    stash_blocks,
    guest_blocks,
    norm_gain,
    query_weight,
    keyval_weight,
    output_weight,
    evict_marks,
):
    sections = lax.axis_size("section")
    section_index = lax.axis_index("section")
    current = activations[0]
    upstream = upstream_grad[0]
    stash_rows = stash_blocks[0]
    guest_rows = guest_blocks[0]
    row_count, model_width = current.shape
    block_count = evict_marks.shape[1]
    block_rows = row_count // block_count
    own_marks = lax.dynamic_index_in_dim(evict_marks, section_index, 0, keepdims=False)
    own_mask = (jnp.repeat(own_marks, block_rows) == 1)[:, None]
    leaving = jnp.where(own_mask, current, jnp.zeros_like(current))
    payload = jnp.stack([guest_rows, leaving])
    bit_total = sections.bit_length() - 1
    bit_order = list(range(bit_total))
    for bit_number in bit_order:
        payload = from_partner(payload, "section", bit_number)
    returned = payload[0]
    arrived = payload[1]
    back_rows = jnp.where(own_mask, returned, stash_rows)
    kept_rows = jnp.where(own_mask, jnp.zeros_like(current), current)
    gain_row = norm_gain[0]
    query_local = query_weight[0]
    keyval_local = keyval_weight[0]
    output_local = output_weight[0]
    query_width = query_local.shape[1]
    keyval_width = keyval_local.shape[2]
    local_kv_heads = keyval_width // HEAD_DIM
    group_size = HEADS // KV_HEADS
    head_scale = HEAD_DIM ** (-0.5)
    keyval_flat = keyval_local.reshape(model_width, 2 * keyval_width)
    normed_now = root_norm(current, gain_row).astype(jnp.bfloat16)
    normed_back = root_norm(back_rows, gain_row).astype(jnp.bfloat16)
    stacked = jnp.stack([normed_now, normed_back, upstream], axis=1)
    fragment = lax.all_gather(stacked, "tensor", axis=0, tiled=True)
    outputs = [
        jnp.dot(fragment[:, 0], query_local, preferred_element_type=jnp.float32),
        jnp.dot(fragment[:, 0], keyval_flat, preferred_element_type=jnp.float32),
        jnp.dot(fragment[:, 1], query_local, preferred_element_type=jnp.float32),
        jnp.dot(fragment[:, 1], keyval_flat, preferred_element_type=jnp.float32),
        jnp.einsum("rd,cd->rc", fragment[:, 2], output_local, preferred_element_type=jnp.float32),
    ]
    projected = jnp.concatenate([result.astype(jnp.bfloat16) for result in outputs], axis=1)
    length = projected.shape[0]
    edge_two = query_width + 2 * keyval_width
    edge_three = edge_two + query_width
    edge_four = edge_three + 2 * keyval_width
    query_now = projected[:, :query_width].reshape(length, local_kv_heads, group_size, HEAD_DIM)
    keyval_now = projected[:, query_width:edge_two].reshape(length, 2, local_kv_heads, HEAD_DIM)
    query_back = projected[:, edge_two:edge_three].reshape(
        length, local_kv_heads, group_size, HEAD_DIM
    )
    keyval_back = projected[:, edge_three:edge_four].reshape(length, 2, local_kv_heads, HEAD_DIM)
    grad_context = projected[:, edge_four:].reshape(length, local_kv_heads, group_size, HEAD_DIM)
    scores_now = jnp.einsum(
        "tkgh,ukh->kgtu", query_now, keyval_now[:, 0], preferred_element_type=jnp.float32
    )
    probs_now = causal_probs(scores_now * head_scale)
    weights_now = probs_now.astype(jnp.bfloat16)
    context_now = jnp.einsum(
        "kgtu,ukh->tkgh", weights_now, keyval_now[:, 1], preferred_element_type=jnp.float32
    )
    context_flat = context_now.astype(jnp.bfloat16).reshape(length, query_width)
    key_back = keyval_back[:, 0]
    value_back = keyval_back[:, 1]
    scores_back = jnp.einsum(
        "tkgh,ukh->kgtu", query_back, key_back, preferred_element_type=jnp.float32
    )
    probs_back = causal_probs(scores_back * head_scale)
    weights_back = probs_back.astype(jnp.bfloat16)
    grad_value = jnp.einsum(
        "kgtu,tkgh->ukh", weights_back, grad_context, preferred_element_type=jnp.float32
    ).astype(jnp.bfloat16)
    grad_prob = jnp.einsum(
        "tkgh,ukh->kgtu", grad_context, value_back, preferred_element_type=jnp.float32
    )
    grad_score = (
        probs_back
        * (grad_prob - jnp.sum(probs_back * grad_prob, axis=-1, keepdims=True))
        * head_scale
    )
    grad_score = grad_score.astype(jnp.bfloat16)
    grad_query = jnp.einsum(
        "kgtu,ukh->tkgh", grad_score, key_back, preferred_element_type=jnp.float32
    )
    grad_query = grad_query.astype(jnp.bfloat16).reshape(length, query_width)
    grad_key = jnp.einsum(
        "kgtu,tkgh->ukh", grad_score, query_back, preferred_element_type=jnp.float32
    ).astype(jnp.bfloat16)
    grad_keyval = jnp.stack([grad_key, grad_value], axis=1).reshape(length, 2, keyval_width)
    forward_term = jnp.dot(context_flat, output_local, preferred_element_type=jnp.float32)
    backward_term = jnp.einsum(
        "tc,dc->td", grad_query, query_local, preferred_element_type=jnp.float32
    )
    backward_term = backward_term + jnp.einsum(
        "tjc,djc->td", grad_keyval, keyval_local, preferred_element_type=jnp.float32
    )
    rounded = lax.optimization_barrier(
        jnp.stack([forward_term, backward_term], axis=1).astype(jnp.bfloat16)
    )
    summed = lax.psum(rounded.astype(jnp.float32).astype(jnp.bfloat16), "tensor").astype(
        jnp.float32
    )
    own_share = lax.dynamic_slice_in_dim(summed, lax.axis_index("tensor") * row_count, row_count, 0)
    updated = (current.astype(jnp.float32) + own_share[:, 0]).astype(jnp.bfloat16)
    normed_out, pull_back = jax.vjp(
        lambda inputs: root_norm(inputs, gain_row), back_rows.astype(jnp.float32)
    )
    norm_grad = pull_back(own_share[:, 1])[0]
    passed = (upstream.astype(jnp.float32) + norm_grad).astype(jnp.bfloat16)
    sent_forward = shifted(updated[None], "section", 1)
    sent_back = shifted(passed[None], "section", -1)
    return (sent_forward, sent_back, kept_rows[None], arrived[None])


def solution(mesh):
    placed = (
        P("section", "tensor", None),
        P("section", "tensor", None),
        P("section", "tensor", None),
        P("section", "tensor", None),
        P("section", None),
        P("section", None, "tensor"),
        P("section", None, None, "tensor"),
        P("section", "tensor", None),
        P(),
    )
    return jax.shard_map(
        local,
        mesh=mesh,
        in_specs=placed,
        out_specs=(
            P("section", "tensor", None),
            P("section", "tensor", None),
            P("section", "tensor", None),
            P("section", "tensor", None),
        ),
        check_vma=False,
    )
```

profile of v0, /device:TPU:2, one launch (start us, length us, event | category | flops | bytes accessed | tf_op | source)
XLA Modules:
  0.0 465.3 jit_solution(203770623586910261)
XLA Ops:
  7.2 0.9 fusion.65
  8.3 1.8 broadcast_select_fusion
  10.0 1.0 pad_maximum_fusion.2
  11.1 1.9 collective-permute-done
  13.0 1.9 collective-permute-start.1
  15.0 12.2 %collective-permute-done.1 = bf16[2,32,4096]{2,1,0:T(8,128)(2,1)S(1)} collective-permute-done((bf16[2,32,4096]{2,1,0:T(8,128)(2,1)S(1)}, bf16[2,32,4096]{2,1,0:T(8,128)(2,1)S(1)}, u32[]{:S(2)}, u32[]{:S(2)}) %collective-permute-start.1) | collective-permute-done | bytes 524320 | tf_op jit(solution)/shard_map/ppermute | solution.py:14
  27.2 3.3 collective-permute-start.2
  30.5 22.8 %collective-permute-done.2 = bf16[2,32,4096]{2,1,0:T(8,128)(2,1)S(1)} collective-permute-done((bf16[2,32,4096]{2,1,0:T(8,128)(2,1)S(1)}, bf16[2,32,4096]{2,1,0:T(8,128)(2,1)S(1)}, u32[]{:S(2)}, u32[]{:S(2)}) %collective-permute-start.2) | collective-permute-done | bytes 524320 | tf_op jit(solution)/shard_map/ppermute | solution.py:14
  53.2 1.3 collective-permute-start.3
  54.5 11.8 %collective-permute-done.3 = bf16[2,32,4096]{2,1,0:T(8,128)(2,1)S(1)} collective-permute-done((bf16[2,32,4096]{2,1,0:T(8,128)(2,1)S(1)}, bf16[2,32,4096]{2,1,0:T(8,128)(2,1)S(1)}, u32[]{:S(2)}, u32[]{:S(2)}) %collective-permute-start.3) | collective-permute-done | bytes 524320 | tf_op jit(solution)/shard_map/ppermute | solution.py:14
  66.3 1.9 collective-permute-start.4
  68.2 1.1 fusion.49
  69.3 10.8 %collective-permute-done.4 = bf16[2,32,4096]{2,1,0:T(8,128)(2,1)S(1)} collective-permute-done((bf16[2,32,4096]{2,1,0:T(8,128)(2,1)S(1)}, bf16[2,32,4096]{2,1,0:T(8,128)(2,1)S(1)}, u32[]{:S(2)}, u32[]{:S(2)}) %collective-permute-start.4) | collective-permute-done | bytes 524320 | tf_op jit(solution)/shard_map/ppermute | solution.py:14
  80.1 1.2 fusion.47
  81.3 1.3 fusion.53
  82.6 1.9 pad_maximum_fusion.1
  84.8 141.7 %all-gather.2.cloned.1.call-done = bf16[256,3,4096]{2,0,1:T(8,128)(2,1)} async-done(((bf16[32,3,4096]{2,0,1:T(8,128)(2,1)}), bf16[256,3,4096]{2,0,1:T(8,128)(2,1)}) %all-gather.2.cloned.1.call-update) | async-done | bytes 6291472 | tf_op jit(solution)/shard_map/all_gather | solution.py:83
  226.5 4.1 fusion.25
  230.7 4.3 fusion.28
  235.2 2.5 fusion.37
  237.7 0.3 fusion.69
  238.2 0.3 fusion.42
  238.6 0.3 multiply_reduce_fusion
  238.9 0.3 fusion.56
  239.2 0.3 fusion.43
  239.8 0.6 slice-done
  240.4 0.8 slice-done.1
  241.2 1.0 fusion.34
  242.2 0.3 copy-done.2
  242.5 1.3 fusion.31
  243.8 0.3 fusion.70
  244.3 0.3 convolution_convert_fusion.2
  244.7 1.3 copy-done
  246.0 1.3 fusion.1
  247.3 0.8 convolution_bitcast_fusion
  248.1 1.3 fusion.2
  249.4 2.3 pad_maximum_fusion
  251.8 191.1 %all-reduce.2.cloned.1.call-done = bf16[256,2,4096]{2,0,1:T(8,128)(2,1)} async-done(((bf16[256,2,4096]{2,0,1:T(8,128)(2,1)}), bf16[256,2,4096]{2,0,1:T(8,128)(2,1)}) %all-reduce.2.cloned.1.call-update) | async-done | bytes 4194320 | tf_op jit(solution)/shard_map/psum | solution.py:149
  442.9 1.1 dynamic-slice_convert_fusion
  444.0 0.3 fusion.48
  444.3 0.3 fusion.55
  444.6 1.9 collective-permute-start.6
  446.5 2.4 collective-permute-start.5
  449.0 0.7 slice.56
  449.7 0.7 collective-permute-done.6
  450.4 6.6 %collective-permute-done.5 = bf16[1,32,4096]{2,1,0:T(8,128)(2,1)S(1)} collective-permute-done((bf16[1,32,4096]{2,1,0:T(8,128)(2,1)S(1)}, bf16[1,32,4096]{2,1,0:T(8,128)(2,1)S(1)}, u32[]{:S(2)}, u32[]{:S(2)}) %collective-permute-start.5) | collective-permute-done | bytes 262176 | tf_op jit(solution)/shard_map/ppermute | solution.py:20
  457.0 0.7 copy.82
  457.7 0.7 copy.83
  (31 shorter events, 1.5 us)
Async XLA Ops:
  7.2 219.4 %all-gather.2.cloned.1.call-start = ((), (), s32[]{:S(2)}) async-start(), calls=%async_computation | async-start | bytes 7077888 | tf_op jit(solution)/shard_map/all_gather | solution.py:83
  11.0 2.0 collective-permute-start
  13.0 14.1 %collective-permute-start.1 = (bf16[2,32,4096]{2,1,0:T(8,128)(2,1)S(1)}, bf16[2,32,4096]{2,1,0:T(8,128)(2,1)S(1)}, u32[]{:S(2)}, u32[]{:S(2)}) collective-permute-start(bf16[2,32,4096]{2,1,0:T(8,128)(2,1)S(1)} %collective-permute-done), channel_id=1, source_target_pairs={{0,16},{8,24},{16,0},{24,8},{32,48},{40,56},{48,32},{56,40},{64,80... | collective-permute-start | bytes 1572872 | tf_op jit(solution)/shard_map/ppermute | solution.py:14
  27.2 26.0 %collective-permute-start.2 = (bf16[2,32,4096]{2,1,0:T(8,128)(2,1)S(1)}, bf16[2,32,4096]{2,1,0:T(8,128)(2,1)S(1)}, u32[]{:S(2)}, u32[]{:S(2)}) collective-permute-start(bf16[2,32,4096]{2,1,0:T(8,128)(2,1)S(1)} %collective-permute-done.1), channel_id=1, source_target_pairs={{0,32},{8,40},{16,48},{24,56},{32,0},{40,8},{48,16},{56,24},{64,96... | collective-permute-start | bytes 1572872 | tf_op jit(solution)/shard_map/ppermute | solution.py:14
  53.2 13.1 %collective-permute-start.3 = (bf16[2,32,4096]{2,1,0:T(8,128)(2,1)S(1)}, bf16[2,32,4096]{2,1,0:T(8,128)(2,1)S(1)}, u32[]{:S(2)}, u32[]{:S(2)}) collective-permute-start(bf16[2,32,4096]{2,1,0:T(8,128)(2,1)S(1)} %collective-permute-done.2), channel_id=1, source_target_pairs={{0,64},{8,72},{16,80},{24,88},{32,96},{40,104},{48,112},{56,120},{... | collective-permute-start | bytes 1572872 | tf_op jit(solution)/shard_map/ppermute | solution.py:14
  66.3 13.7 %collective-permute-start.4 = (bf16[2,32,4096]{2,1,0:T(8,128)(2,1)S(1)}, bf16[2,32,4096]{2,1,0:T(8,128)(2,1)S(1)}, u32[]{:S(2)}, u32[]{:S(2)}) collective-permute-start(bf16[2,32,4096]{2,1,0:T(8,128)(2,1)S(1)} %collective-permute-done.3), channel_id=1, source_target_pairs={{0,128},{8,136},{16,144},{24,152},{32,160},{40,168},{48,176},{56,1... | collective-permute-start | bytes 1572872 | tf_op jit(solution)/shard_map/ppermute | solution.py:14
  84.5 358.4 %all-reduce.2.cloned.1.call-start = ((), (), s32[]{:S(2)}) async-start(), calls=%async_computation.1 | async-start | bytes 8388608 | tf_op jit(solution)/shard_map/psum | solution.py:149
  230.7 4.4 copy-start.4
  238.2 2.2 slice-start
  238.6 2.6 slice-start.1
  239.2 3.3 copy-start.2
  243.8 2.2 copy-start
  251.7 192.3 %copy-start.1 = (bf16[1,32,4096]{2,1,0:T(8,128)(2,1)S(1)}, bf16[1,32,4096]{2,1,0:T(8,128)(2,1)}, u32[]{:S(2)}) copy-start(bf16[1,32,4096]{2,1,0:T(8,128)(2,1)} %param.11) | copy-start | bytes 786436
  251.7 192.3 %copy-start.6 = (f32[1,4096]{1,0:T(1,128)S(1)}, f32[1,4096]{1,0:T(1,128)}, u32[]{:S(2)}) copy-start(f32[1,4096]{1,0:T(1,128)} %param.13) | copy-start | bytes 49156
  251.7 192.6 %copy-start.3 = (bf16[1,32,4096]{2,1,0:T(8,128)(2,1)S(1)}, bf16[1,32,4096]{2,1,0:T(8,128)(2,1)}, u32[]{:S(2)}) copy-start(bf16[1,32,4096]{2,1,0:T(8,128)(2,1)} %param.9) | copy-start | bytes 786436
  251.7 192.6 %copy-start.5 = (bf16[1,32,4096]{2,1,0:T(8,128)(2,1)S(1)}, bf16[1,32,4096]{2,1,0:T(8,128)(2,1)}, u32[]{:S(2)}) copy-start(bf16[1,32,4096]{2,1,0:T(8,128)(2,1)} %param.10) | copy-start | bytes 786436
  444.6 5.8 %collective-permute-start.6 = (bf16[1,32,4096]{2,1,0:T(8,128)(2,1)S(1)}, bf16[1,32,4096]{2,1,0:T(8,128)(2,1)S(1)}, u32[]{:S(2)}, u32[]{:S(2)}) collective-permute-start(bf16[1,32,4096]{2,1,0:T(8,128)(2,1)S(1)} %get-tuple-element.4), channel_id=1, source_target_pairs={{8,0},{16,8},{24,16},{32,24},{40,32},{48,40},{56,48},{64,56},{72,6... | collective-permute-start | bytes 786440 | tf_op jit(solution)/shard_map/ppermute | solution.py:20
  446.5 10.5 %collective-permute-start.5 = (bf16[1,32,4096]{2,1,0:T(8,128)(2,1)S(1)}, bf16[1,32,4096]{2,1,0:T(8,128)(2,1)S(1)}, u32[]{:S(2)}, u32[]{:S(2)}) collective-permute-start(bf16[1,32,4096]{2,1,0:T(8,128)(2,1)S(1)} %get-tuple-element.5), channel_id=1, source_target_pairs={{0,8},{8,16},{16,24},{24,32},{32,40},{40,48},{48,56},{56,64},{64,7... | collective-permute-start | bytes 786440 | tf_op jit(solution)/shard_map/ppermute | solution.py:20
Sparse Core Ops, SparseCore 0:
  84.6 141.8 all-gather.1
  251.9 190.9 all-reduce.1
where the time goes:
time: 466 us; the launch traced here: 465 us
  waiting for transfers between devices  400 us (86%)
  matrix products  18.8 us (4%)
  between operations  14.3 us (3%)
  other arithmetic  13.8 us (3%)
  starting transfers between devices  13 us (3%)
  local copies, waits for them, and re-layouts  5.6 us (1%)
    psum x1, waiting for transfers between devices, local(): lax.psum(rounded.astype(jnp.float32).astype(jnp.bfloat16), 'tensor')  191 us
    all_gather x1, waiting for transfers between devices, local(): fragment = lax.all_gather(stacked, 'tensor', axis=0, tiled=True)  142 us
    ppermute x5, waiting for transfers between devices, from_partner(): lax.ppermute(x, axis, [(i, i ^ 1 << bit) for i in range(lax.axis_size(axi...  59.5 us
  transfers between devices with their start and end apart: 9, of which 9 were waited for; matrix products, arithmetic and copies ran while one was open for 0% of the time, Pallas kernels for 0%

commit v1 on v0

--- a/solution.py
+++ b/solution.py
@@ -146,9 +146,9 @@
     rounded = lax.optimization_barrier(
         jnp.stack([forward_term, backward_term], axis=1).astype(jnp.bfloat16)
     )
-    summed = lax.psum(rounded.astype(jnp.float32).astype(jnp.bfloat16), "tensor").astype(
-        jnp.float32
-    )
+    summed = jnp.sum(
+        lax.all_gather(rounded.astype(jnp.float32).astype(jnp.bfloat16), "tensor"), axis=0
+    ).astype(jnp.float32)
     own_share = lax.dynamic_slice_in_dim(summed, lax.axis_index("tensor") * row_count, row_count, 0)
     updated = (current.astype(jnp.float32) + own_share[:, 0]).astype(jnp.bfloat16)
     normed_out, pull_back = jax.vjp(

time: 466 us -> 858 us (1.84)
  waiting for transfers between devices: 400 us -> 774 us
  other arithmetic: 13.8 us -> 28.1 us
    all_gather x0 -> x1, waiting for transfers between devices: none -> 569 us  [local(): lax.all_gather(rounded.astype(jnp.float32).astype(jnp.bfloat16), 'tensor')]
    psum x1 -> x0, waiting for transfers between devices: 191 us -> none  [local(): lax.psum(rounded.astype(jnp.float32).astype(jnp.bfloat16), 'tensor')]
    reduce_sum x0 -> x1, other arithmetic: none -> 14.2 us  [local(): jnp.sum(lax.all_gather(rounded.astype(jnp.float32).astype(jnp.bfloat16),...]
where the time goes in v1:
time: 858 us; the launch traced here: 857 us
  waiting for transfers between devices  774 us (90%)
  other arithmetic  28.1 us (3%)
  matrix products  18.9 us (2%)
  starting transfers between devices  16.9 us (2%)
  between operations  14.3 us (2%)
    all_gather x1, waiting for transfers between devices, local(): lax.all_gather(rounded.astype(jnp.float32).astype(jnp.bfloat16), 'tensor')  569 us
    all_gather x1, waiting for transfers between devices, local(): fragment = lax.all_gather(stacked, 'tensor', axis=0, tiled=True)  142 us
    ppermute x5, waiting for transfers between devices, from_partner(): lax.ppermute(x, axis, [(i, i ^ 1 << bit) for i in range(lax.axis_size(axi...  59.5 us
  transfers between devices with their start and end apart: 9, of which 9 were waited for; matrix products, arithmetic and copies ran while one was open for 0% of the time, Pallas kernels for 0%

profile of v1, /device:TPU:2, one launch (start us, length us, event | category | flops | bytes accessed | tf_op | source)
XLA Modules:
  0.0 857.2 jit_solution(10703864272888846324)
XLA Ops:
  7.2 0.9 fusion.65
  8.3 1.8 broadcast_select_fusion
  10.0 1.0 pad_maximum_fusion.2
  11.1 1.9 collective-permute-done
  13.0 1.9 collective-permute-start.1
  15.0 12.2 %collective-permute-done.1 = bf16[2,32,4096]{2,1,0:T(8,128)(2,1)S(1)} collective-permute-done((bf16[2,32,4096]{2,1,0:T(8,128)(2,1)S(1)}, bf16[2,32,4096]{2,1,0:T(8,128)(2,1)S(1)}, u32[]{:S(2)}, u32[]{:S(2)}) %collective-permute-start.1) | collective-permute-done | bytes 524320 | tf_op jit(solution)/shard_map/ppermute | solution.py:14
  27.2 3.3 collective-permute-start.2
  30.5 22.8 %collective-permute-done.2 = bf16[2,32,4096]{2,1,0:T(8,128)(2,1)S(1)} collective-permute-done((bf16[2,32,4096]{2,1,0:T(8,128)(2,1)S(1)}, bf16[2,32,4096]{2,1,0:T(8,128)(2,1)S(1)}, u32[]{:S(2)}, u32[]{:S(2)}) %collective-permute-start.2) | collective-permute-done | bytes 524320 | tf_op jit(solution)/shard_map/ppermute | solution.py:14
  53.2 1.3 collective-permute-start.3
  54.5 11.8 %collective-permute-done.3 = bf16[2,32,4096]{2,1,0:T(8,128)(2,1)S(1)} collective-permute-done((bf16[2,32,4096]{2,1,0:T(8,128)(2,1)S(1)}, bf16[2,32,4096]{2,1,0:T(8,128)(2,1)S(1)}, u32[]{:S(2)}, u32[]{:S(2)}) %collective-permute-start.3) | collective-permute-done | bytes 524320 | tf_op jit(solution)/shard_map/ppermute | solution.py:14
  66.3 1.9 collective-permute-start.4
  68.2 1.1 fusion.49
  69.3 10.8 %collective-permute-done.4 = bf16[2,32,4096]{2,1,0:T(8,128)(2,1)S(1)} collective-permute-done((bf16[2,32,4096]{2,1,0:T(8,128)(2,1)S(1)}, bf16[2,32,4096]{2,1,0:T(8,128)(2,1)S(1)}, u32[]{:S(2)}, u32[]{:S(2)}) %collective-permute-start.4) | collective-permute-done | bytes 524320 | tf_op jit(solution)/shard_map/ppermute | solution.py:14
  80.1 1.2 fusion.47
  81.3 1.3 fusion.53
  82.6 1.9 pad_maximum_fusion.1
  84.8 141.7 %all-gather.4.cloned.1.call-done = bf16[256,3,4096]{2,0,1:T(8,128)(2,1)} async-done(((bf16[32,3,4096]{2,0,1:T(8,128)(2,1)}), bf16[256,3,4096]{2,0,1:T(8,128)(2,1)}) %all-gather.4.cloned.1.call-update) | async-done | bytes 6291472 | tf_op jit(solution)/shard_map/all_gather | solution.py:83
  226.5 4.1 fusion.25
  230.7 4.3 fusion.28
  235.2 2.7 fusion.37
  237.8 0.3 fusion.69
  238.4 0.3 multiply_reduce_fusion
  238.7 0.3 fusion.56
  239.0 0.2 convolution_convert_fusion.1
  239.3 0.3 fusion.43
  239.6 0.3 fusion.42
  240.0 1.3 copy-done.2
  241.3 1.2 fusion.31
  242.5 1.0 fusion.34
  243.6 0.4 fusion.70
  244.1 0.3 convolution_convert_fusion.2
  244.4 1.3 copy-done
  245.7 1.3 fusion.1
  247.1 0.8 convolution_bitcast_fusion
  247.8 1.3 fusion.2
  249.2 2.4 pad_maximum_fusion
  251.6 569.3 %all-gather.6.cloned.1.call-done = bf16[2048,2,4096]{2,0,1:T(8,128)(2,1)} async-done(((bf16[256,2,4096]{2,0,1:T(8,128)(2,1)}), bf16[2048,2,4096]{2,0,1:T(8,128)(2,1)}) %all-gather.6.cloned.1.call-update) | async-done | bytes 33554448 | tf_op jit(solution)/shard_map/all_gather | solution.py:150
  820.9 14.2 %reduce_sum.79 = bf16[256,2,4096]{2,0,1:T(8,128)(2,1)} reduce(bf16[8,256,2,4096]{3,1,0,2:T(8,128)(2,1)} %bitcast.218, bf16[]{:T(256)} %constant.34.clone.1), dimensions={0}, to_apply=%region_7.8 | reduce | flops 14680064 | bytes 37748736 | tf_op jit(solution)/shard_map/reduce_sum | solution.py:149
  835.1 1.1 dynamic-slice_convert_fusion
  836.2 0.3 fusion.48
  836.5 0.3 fusion.55
  836.8 1.9 collective-permute-start.5
  838.7 6.3 collective-permute-start.6
  845.1 0.7 slice.56
  845.8 1.5 collective-permute-done.5
  847.3 1.7 collective-permute-done.6
  849.0 0.7 copy.81
  849.7 0.7 copy.82
  (32 shorter events, 1.3 us)
Async XLA Ops:
  7.2 219.4 %all-gather.4.cloned.1.call-start = ((), (), s32[]{:S(2)}) async-start(), calls=%async_computation | async-start | bytes 7077888 | tf_op jit(solution)/shard_map/all_gather | solution.py:83
  11.0 2.0 collective-permute-start
  13.0 14.1 %collective-permute-start.1 = (bf16[2,32,4096]{2,1,0:T(8,128)(2,1)S(1)}, bf16[2,32,4096]{2,1,0:T(8,128)(2,1)S(1)}, u32[]{:S(2)}, u32[]{:S(2)}) collective-permute-start(bf16[2,32,4096]{2,1,0:T(8,128)(2,1)S(1)} %collective-permute-done), channel_id=1, source_target_pairs={{0,16},{8,24},{16,0},{24,8},{32,48},{40,56},{48,32},{56,40},{64,80... | collective-permute-start | bytes 1572872 | tf_op jit(solution)/shard_map/ppermute | solution.py:14
  27.2 26.0 %collective-permute-start.2 = (bf16[2,32,4096]{2,1,0:T(8,128)(2,1)S(1)}, bf16[2,32,4096]{2,1,0:T(8,128)(2,1)S(1)}, u32[]{:S(2)}, u32[]{:S(2)}) collective-permute-start(bf16[2,32,4096]{2,1,0:T(8,128)(2,1)S(1)} %collective-permute-done.1), channel_id=1, source_target_pairs={{0,32},{8,40},{16,48},{24,56},{32,0},{40,8},{48,16},{56,24},{64,96... | collective-permute-start | bytes 1572872 | tf_op jit(solution)/shard_map/ppermute | solution.py:14
  53.2 13.1 %collective-permute-start.3 = (bf16[2,32,4096]{2,1,0:T(8,128)(2,1)S(1)}, bf16[2,32,4096]{2,1,0:T(8,128)(2,1)S(1)}, u32[]{:S(2)}, u32[]{:S(2)}) collective-permute-start(bf16[2,32,4096]{2,1,0:T(8,128)(2,1)S(1)} %collective-permute-done.2), channel_id=1, source_target_pairs={{0,64},{8,72},{16,80},{24,88},{32,96},{40,104},{48,112},{56,120},{... | collective-permute-start | bytes 1572872 | tf_op jit(solution)/shard_map/ppermute | solution.py:14
  66.3 13.7 %collective-permute-start.4 = (bf16[2,32,4096]{2,1,0:T(8,128)(2,1)S(1)}, bf16[2,32,4096]{2,1,0:T(8,128)(2,1)S(1)}, u32[]{:S(2)}, u32[]{:S(2)}) collective-permute-start(bf16[2,32,4096]{2,1,0:T(8,128)(2,1)S(1)} %collective-permute-done.3), channel_id=1, source_target_pairs={{0,128},{8,136},{16,144},{24,152},{32,160},{40,168},{48,176},{56,1... | collective-permute-start | bytes 1572872 | tf_op jit(solution)/shard_map/ppermute | solution.py:14
  84.5 736.4 %all-gather.6.cloned.1.call-start = ((), (), s32[]{:S(2)}) async-start(), calls=%async_computation.1 | async-start | bytes 37748736 | tf_op jit(solution)/shard_map/all_gather | solution.py:150
  230.7 4.4 copy-start.4
  235.2 4.8 slice-start
  238.4 1.6 slice-start.1
  238.7 2.6 copy-start.2
  243.6 2.2 copy-start
  820.9 15.3 %copy-start.1 = (bf16[1,32,4096]{2,1,0:T(8,128)(2,1)S(1)}, bf16[1,32,4096]{2,1,0:T(8,128)(2,1)}, u32[]{:S(2)}) copy-start(bf16[1,32,4096]{2,1,0:T(8,128)(2,1)} %param.11) | copy-start | bytes 786436
  820.9 15.3 %copy-start.6 = (f32[1,4096]{1,0:T(1,128)S(1)}, f32[1,4096]{1,0:T(1,128)}, u32[]{:S(2)}) copy-start(f32[1,4096]{1,0:T(1,128)} %param.13) | copy-start | bytes 49156
  820.9 15.6 %copy-start.3 = (bf16[1,32,4096]{2,1,0:T(8,128)(2,1)S(1)}, bf16[1,32,4096]{2,1,0:T(8,128)(2,1)}, u32[]{:S(2)}) copy-start(bf16[1,32,4096]{2,1,0:T(8,128)(2,1)} %param.9) | copy-start | bytes 786436
  820.9 15.6 %copy-start.5 = (bf16[1,32,4096]{2,1,0:T(8,128)(2,1)S(1)}, bf16[1,32,4096]{2,1,0:T(8,128)(2,1)}, u32[]{:S(2)}) copy-start(bf16[1,32,4096]{2,1,0:T(8,128)(2,1)} %param.10) | copy-start | bytes 786436
  836.8 10.5 %collective-permute-start.5 = (bf16[1,32,4096]{2,1,0:T(8,128)(2,1)S(1)}, bf16[1,32,4096]{2,1,0:T(8,128)(2,1)S(1)}, u32[]{:S(2)}, u32[]{:S(2)}) collective-permute-start(bf16[1,32,4096]{2,1,0:T(8,128)(2,1)S(1)} %get-tuple-element.5), channel_id=1, source_target_pairs={{0,8},{8,16},{16,24},{24,32},{32,40},{40,48},{48,56},{56,64},{64,7... | collective-permute-start | bytes 786440 | tf_op jit(solution)/shard_map/ppermute | solution.py:20
  838.7 10.2 %collective-permute-start.6 = (bf16[1,32,4096]{2,1,0:T(8,128)(2,1)S(1)}, bf16[1,32,4096]{2,1,0:T(8,128)(2,1)S(1)}, u32[]{:S(2)}, u32[]{:S(2)}) collective-permute-start(bf16[1,32,4096]{2,1,0:T(8,128)(2,1)S(1)} %get-tuple-element.4), channel_id=1, source_target_pairs={{8,0},{16,8},{24,16},{32,24},{40,32},{48,40},{56,48},{64,56},{72,6... | collective-permute-start | bytes 786440 | tf_op jit(solution)/shard_map/ppermute | solution.py:20
Sparse Core Ops, SparseCore 0:
  84.6 141.8 all-gather.3
  251.7 569.1 all-gather.5
